TPU v7x, 256 devices: a whole 4x4x8 slice. The times are simulated.
256 devices in a mesh: harm: 8 (over x, y_lo), dom: 32 (over y_hi, z, core).
Axes of the slice: x: 4, y: 4 (y_hi: 2, y_lo: 2; y = y_hi * 2 + y_lo), z: 8, core: 2. Of those that a mesh axis runs over, the one named last changes fastest.
Arguments:
- response: float32 [2, 64, 64, 8192], P(None, 'harm', None, 'dom'), may hold values from -6 to 6
- base_coeff: float32 [2, 17, 64, 8192], P(None, None, None, 'dom'), may hold values from -1.5 to 1.5
- volume_mat: float32 [64, 64], replicated, may hold values from -0.75 to 0.75
- trace_mats: float32 [4, 16, 64], replicated, may hold values from -0.75 to 0.75
- lift_mat: float32 [64, 16], replicated, may hold values from -1.5 to 1.5
- round_masks: int32 [4], replicated, may hold values from 1 to 31, as said below
- send_elem: int32 [4, 2048], P(None, 'dom'), may hold values from 0 to 255
- send_face: int32 [4, 2048], P(None, 'dom'), may hold values from 0 to 3
- recv_elem: int32 [4, 2048], P(None, 'dom'), may hold values from 0 to 255
Outputs:
- image: float32 [2, 64, 64, 8192], P(None, 'harm', None, 'dom')
Inputs may be any that keep to these rules, and one draw needn't show every extreme that they name: `round_masks`: 4 distinct masks, among them the smallest and the largest possible mask; in each round partition p is matched with partition p XOR mask.
All inputs are finite; a program needn't handle non-finite values.
Results may differ from a plain program's by a relative error of at most 0.0001.
Values sent between devices are 32-bit elements; how exact they have to be, the bound alone decides.
No kernel may reach another device: no remote copies, remote signals or barrier semaphores. Data moves between devices by JAX's collectives and lax.ppermute only.
A program may use at most 64 MiB of HBM per device.

v0:
```python
import functools

import jax
import jax.numpy as jnp
from jax import lax
from jax.experimental import pallas as pl
from jax.experimental.pallas import tpu as pltpu
from jax.sharding import PartitionSpec as P


REACH = 8
ROUNDS = 4
WIDTHS = (2, 2, 2, 2)
EARLY = 2
base_omega = 0.2

F32 = jnp.float32
BF16 = jnp.bfloat16
KERNEL_MEMORY = pltpu.CompilerParams(vmem_limit_bytes=8 * 2**20)
HBM = pl.BlockSpec(memory_space=pl.ANY)
VMEM = pl.BlockSpec(memory_space=pltpu.VMEM)
SMEM = pl.BlockSpec(memory_space=pltpu.SMEM)


def split(value):
    high = value.astype(BF16)
    low = (value - high.astype(F32)).astype(BF16)
    return high, low


def dot(a, b):
    return lax.dot_general(a, b, (((1,), (0,)), ((), ())), preferred_element_type=F32)


def dot_nt(a, b):
    return lax.dot_general(a, b, (((1,), (1,)), ((), ())), preferred_element_type=F32)


def round_rows(masks):
    first = jnp.int32(0)
    last = jnp.int32(0)
    for r in range(ROUNDS):
        smallest = masks[r] == 1
        largest = masks[r] == 31
        first = jnp.where(smallest, r, first)
        last = jnp.where(largest, r, last)
    mid_a = jnp.int32(0)
    mid_b = jnp.int32(0)
    for r in range(ROUNDS):
        middle = jnp.logical_and(first != r, last != r)
        mid_b = jnp.where(middle, r, mid_b)
        back = ROUNDS - 1 - r
        middle = jnp.logical_and(first != back, last != back)
        mid_a = jnp.where(middle, back, mid_a)
    return first, last, mid_a, mid_b


def slot_row(ref, rows):
    return jnp.concatenate([ref[pl.ds(r, 1), :] for r in rows], axis=1)


def piece_copy(response, k, piece, sem):
    count = response.shape[1]
    odd = lax.axis_index("harm") % 2
    upward, downward = (chunk_harmonics(k, count, way)[0] for way in (True, False))
    first = jnp.where(odd == 1, downward, upward)
    return pltpu.make_async_copy(response.at[:, pl.ds(first, WIDTHS[k])], piece, sem)


def cut_kernel(response, piece, sem):
    copy = piece_copy(response, 0, piece, sem)
    copy.start()
    copy.wait()


def trace_kernel(masks_hbm, response_hbm, coeff_hbm, mats_hbm, elem_hbm, face_hbm, recv_hbm, *refs):
    count = len(WIDTHS) - 1
    first, lane_bits, places, response, coeff = refs[:5]
    pieces = refs[5:5 + count]
    p_high, p_low, masks, trace_mats, send_elem, send_face, recv_elem, sems = refs[5 + count:]
    fetched = (
        (response_hbm, response), (masks_hbm, masks), (elem_hbm, send_elem), (face_hbm, send_face),
        (mats_hbm, trace_mats), (recv_hbm, recv_elem),
    )
    fetches = [
        pltpu.make_async_copy(source, target, sems.at[n]) for n, (source, target) in enumerate(fetched)
    ]
    copies = [
        piece_copy(response_hbm, k, piece, sems.at[len(fetched) + k])
        for k, piece in enumerate(pieces, 1)
    ]
    copies.append(pltpu.make_async_copy(coeff_hbm, coeff, sems.at[len(fetched)]))
    for copy in fetches + copies:
        copy.start()
    for copy in fetches[1:]:
        copy.wait()
    rows = round_rows(masks)
    elems = slot_row(send_elem, rows)
    faces = slot_row(send_face, rows)
    places[0:1, :] = slot_row(recv_elem, rows)
    harm_count, unknowns, elements = response.shape[1:]
    slots = elems.shape[1]
    half = slots // 4
    pick = (lax.broadcasted_iota(jnp.int32, (elements, slots), 0) == elems).astype(F32).astype(BF16)
    mats = trace_mats[...].reshape(-1, unknowns)
    m_high, m_low = split(mats)
    stack = jnp.concatenate([m_high, m_low, m_high], axis=1)
    face_vars = mats.shape[0] // 4
    left = lax.broadcasted_iota(jnp.int32, (face_vars, 2 * half), 1) < half
    for n, row in enumerate(rows[2:]):
        mask = jnp.full((1, 2 * half), masks[row], jnp.int32)
        bits = [jnp.bitwise_and(jnp.right_shift(mask, b), 1) for b in range(5)]
        bits[2] = jnp.bitwise_xor(bits[2], bits[3])
        for b, bit in enumerate(bits):
            lane_bits[8 * n + b:8 * n + b + 1, :] = bit
    fetches[0].wait()
    high, low = split(response[...].reshape(-1, elements))
    p_high[...] = dot(high, pick).astype(BF16)
    p_low[...] = dot(low, pick).astype(BF16)

    def traced(c, j):
        at = pl.ds((c * harm_count + j) * unknowns, unknowns)
        top = p_high[at, :]
        out = dot(stack, jnp.concatenate([top, top, p_low[at, :]], axis=0))
        total = jnp.zeros((face_vars, slots), F32)
        for face_id in range(4):
            total = total + jnp.where(
                faces == face_id, out[face_id * face_vars:(face_id + 1) * face_vars], 0.0
            )
        return total

    for j in range(harm_count):
        real = traced(0, j)
        imag = traced(1, j)
        ends_r, ends_i = real[:, :2 * half], imag[:, :2 * half]
        mid_r, mid_i = real[:, 2 * half:], imag[:, 2 * half:]
        first[j] = jnp.where(left, mid_r, pltpu.roll(mid_i, half, 1))
        first[harm_count + j] = jnp.where(left, pltpu.roll(mid_r, half, 1), mid_i)
        first[2 * harm_count + j] = jnp.where(left, ends_r, pltpu.roll(ends_i, half, 1))
        first[3 * harm_count + j] = jnp.where(left, pltpu.roll(ends_r, half, 1), ends_i)
    for copy in copies:
        copy.wait()


def choose(lane_bits, chain, row, swapped, kept):
    bit = lane_bits[8 * chain + row:8 * chain + row + 1, :] == 1
    return jnp.where(bit, swapped, kept)


def split_kernel(lane_bits, swapped, kept, out_x, out_y):
    count = out_y.shape[0]
    for n in range(count):
        out_x[n] = choose(lane_bits, 0, 0, swapped[n], kept[n])
        out_y[n] = choose(lane_bits, 1, 0, swapped[count + n], kept[count + n])
    out_x[count:] = swapped[3 * count:]


def first_x_kernel(row, lane_bits, swapped, kept, out, rider):
    count = out.shape[0]
    for n in range(count):
        out[n] = choose(lane_bits, 0, row, swapped[n], kept[n])
    rider[...] = swapped[count:]


def second_x_kernel(row, lane_bits, swapped, kept, rider, out):
    count = kept.shape[0]
    for n in range(count):
        out[n] = choose(lane_bits, 0, row, swapped[n], kept[n])
    out[count:] = rider[...]


def y_kernel(row, lane_bits, swapped, kept, out):
    for n in range(kept.shape[0]):
        out[n] = choose(lane_bits, 1, row, swapped[n], kept[n])


def join_kernel(rows, lane_bits, swapped_x, kept_x, swapped_y, kept_y, out):
    count = kept_y.shape[0]
    for n in range(count):
        out[n] = choose(lane_bits, 0, rows[0], swapped_x[n], kept_x[n])
        out[count + n] = choose(lane_bits, 1, rows[1], swapped_y[n], kept_y[n])
    out[2 * count:] = swapped_x[count:]


def tiles(unknowns, elements, body):
    cols = elements // 128

    def step(t, carry):
        r = pl.ds(pl.multiple_of((t // cols) * 8, 8), 8)
        e = pl.ds(pl.multiple_of((t % cols) * 128, 128), 128)
        body(r, e)
        return carry

    lax.fori_loop(0, (unknowns // 8) * cols, step, 0)


def add_pair(coeff, m, r, e, x, total):
    c_r = coeff[0, m, r, e]
    c_i = coeff[1, m, r, e]
    add_r = c_r * x[0] - c_i * x[1]
    add_i = c_r * x[1] + c_i * x[0]
    if total is None:
        return add_r, add_i
    return total[0] + add_r, total[1] + add_i


def above(i, j):
    return j - i if i <= j else None


def below(i, j):
    return 2 * REACH + j - i if i >= j else None


def inside(i, j):
    return REACH + j - i


def chunk_harmonics(k, count, ascending):
    done = sum(WIDTHS[:k])
    first = done if ascending else count - done - WIDTHS[k]
    return [first + q for q in range(WIDTHS[k])]


def gather_sources(chunks, first, count, ascending, index):
    return [
        (chunk, q, i, index)
        for k, chunk in enumerate(chunks)
        for q, i in enumerate(chunk_harmonics(first + k, count, ascending))
    ]


def convolve(coeff, sources, r, e, start, outputs):
    values = {}
    for j in outputs:
        total = start(j)
        for n, (ref, at, i, index) in enumerate(sources):
            m = index(i, j)
            if m is None:
                continue
            if n not in values:
                values[n] = (ref[0, at, r, e], ref[1, at, r, e])
            total = add_pair(coeff, m, r, e, values[n], total)
        yield j, total


def by_parity(run):
    odd = lax.axis_index("harm") % 2

    @pl.when(odd == 0)
    def _():
        run(False, above, below)

    @pl.when(odd == 1)
    def _():
        run(True, below, above)


def own_kernel(response, coeff, acc):
    harm_count, unknowns, elements = response.shape[1:]
    sources = [(response, i, i, inside) for i in range(harm_count)]

    def body(r, e):
        for j, total in convolve(coeff, sources, r, e, lambda j: None, range(harm_count)):
            acc[0, j, r, e], acc[1, j, r, e] = total

    tiles(unknowns, elements, body)


def near_kernel(first, coeff, acc, *refs):
    chunks, out = refs[:-1], refs[-1]
    harm_count, unknowns, elements = acc.shape[1:]

    def run(ascending, near_index, far_index):
        sources = gather_sources(chunks, first, harm_count, ascending, near_index)

        def body(r, e):
            start = lambda j: (acc[0, j, r, e], acc[1, j, r, e])
            for j, total in convolve(coeff, sources, r, e, start, range(harm_count)):
                out[0, j, r, e], out[1, j, r, e] = total

        tiles(unknowns, elements, body)

    by_parity(run)


def stacked(mat):
    high, low = split(mat)
    return jnp.concatenate([high, low, high], axis=1)


def product(stack, value):
    high, low = split(value)
    return dot(stack, jnp.concatenate([high, high, low], axis=0))


def main_kernel(coeff, response, acc, volume_mat, *refs):
    chunks, out, conv = refs[:-2], refs[-2], refs[-1]
    harm_count, unknowns, elements = acc.shape[1:]

    def run(ascending, near_index, far_index):
        sources = gather_sources(chunks, 0, harm_count, ascending, far_index)

        def body(r, e):
            start = lambda j: (acc[0, j, r, e], acc[1, j, r, e])
            for j, total in convolve(coeff, sources, r, e, start, range(harm_count)):
                conv[0, j, r, e], conv[1, j, r, e] = total

        tiles(unknowns, elements, body)

    by_parity(run)
    stack = stacked(volume_mat[...])
    harm = lax.axis_index("harm")
    period = lax.axis_size("harm") * harm_count
    for j in range(harm_count):
        slot = harm * harm_count + j
        wave = jnp.where(slot < period // 2, slot, slot - period).astype(F32)
        frequency = base_omega * wave
        out[0, j] = product(stack, conv[0, j]) - frequency * response[1, j]
        out[1, j] = product(stack, conv[1, j]) + frequency * response[0, j]


def lift_kernel(
    image, lift_rows, places, lane_bits, small, swapped, kept,
    out, got, done, sems,
):
    harm_count, _, elements = image.shape[1:]
    elems = places[0:1, :]
    slots = elems.shape[1]
    half = slots // 4
    place = (lax.broadcasted_iota(jnp.int32, (elements, slots), 0) == elems).astype(F32).astype(BF16)
    face_vars = lift_rows.shape[0]
    left = lax.broadcasted_iota(jnp.int32, (face_vars, 2 * half), 1) < half
    for j in range(harm_count):
        a = choose(lane_bits, 0, 4, swapped[j], kept[j])
        b = choose(lane_bits, 1, 4, swapped[harm_count + j], kept[harm_count + j])
        for first, second, lanes in (
            (small[2 * harm_count + j], swapped[2 * harm_count + j], slice(0, 2 * half)), (a, b, slice(2 * half, slots))
        ):
            got[pl.ds(j * face_vars, face_vars), lanes] = jnp.where(
                left, first, pltpu.roll(second, half, 1)
            )
            got[pl.ds((harm_count + j) * face_vars, face_vars), lanes] = jnp.where(
                left, pltpu.roll(first, half, 1), second
            )
    g_high, g_low = split(got[...])
    got[...] = dot_nt(g_high, place) + dot_nt(g_low, place)
    l_high, l_low = split(lift_rows[...])
    stack = jnp.concatenate([l_high, l_low, l_high], axis=0)
    copies = []
    for j in range(harm_count):
        for c in range(2):
            at = pl.ds((c * harm_count + j) * face_vars, face_vars)
            q_high, q_low = split(got[at, :])
            done[c, j] = image[c, j] + lax.dot_general(
                stack, jnp.concatenate([q_high, q_high, q_low], axis=0),
                (((0,), (0,)), ((), ())), preferred_element_type=F32,
            )
        copies.append(pltpu.make_async_copy(done.at[:, pl.ds(j, 1)], out.at[:, pl.ds(j, 1)], sems.at[j]))
        copies[-1].start()
    for copy in copies:
        copy.wait()


def edge_kernel(coeff, volume_mat, chunk, image, out, conv):
    width, unknowns, elements = chunk.shape[1:]
    harm_count = out.shape[1]
    last = len(WIDTHS) - 1
    stack = stacked(volume_mat[...])

    def run(ascending, near_index, far_index):
        sources = gather_sources([chunk], last, harm_count, ascending, far_index)
        first = harm_count - width if ascending else 0
        outputs = range(first, first + width)

        def body(r, e):
            for j, total in convolve(coeff, sources, r, e, lambda j: None, outputs):
                conv[0, j - first, r, e], conv[1, j - first, r, e] = total

        tiles(unknowns, elements, body)
        for q in range(width):
            for c in range(2):
                out[c, first + q] = image[c, first + q] + product(stack, conv[c, q])

    by_parity(run)


def resident(*values):
    return [pltpu.with_memory_space_constraint(value, pltpu.VMEM) for value in values]


def stay(*values):
    return [pltpu.with_memory_space_constraint(value, pltpu.HBM) for value in values]


def resident_shape(shape, dtype=F32):
    return pltpu.VMEM(shape, dtype)


def from_partner(value, axis, mask):
    return lax.ppermute(value, axis, [(i, i ^ mask) for i in range(lax.axis_size(axis))])


def shape_like(value):
    return jax.ShapeDtypeStruct(value.shape, value.dtype)


def local(
    response,
    base_coeff,
    volume_mat,
    trace_mats,
    lift_mat,
    round_masks,
    send_elem,
    send_face,
    recv_elem,
):
    harm_count, unknowns, elements = response.shape[1:]
    groups = lax.axis_size("harm")
    skip = [(i, (i + 2) % groups if i % 2 == 0 else (i - 2) % groups) for i in range(groups)]
    near, far = [], []
    whole = response
    face_vars = trace_mats.shape[1]
    slots = send_elem.shape[1]
    piece = pl.pallas_call(
        cut_kernel,
        name="cut",
        compiler_params=KERNEL_MEMORY,
        in_specs=[HBM],
        out_specs=VMEM,
        out_shape=resident_shape((2, WIDTHS[0], unknowns, elements)),
        scratch_shapes=[pltpu.SemaphoreType.DMA],
    )(*stay(response))
    later = len(WIDTHS) - 1
    first, lane_bits, places, response, base_coeff, *pieces = pl.pallas_call(
        trace_kernel,
        name="traces",
        compiler_params=KERNEL_MEMORY,
        in_specs=[HBM] * 7,
        out_specs=[VMEM] * (5 + later),
        out_shape=[
            resident_shape((4 * harm_count, face_vars, 2 * slots)),
            resident_shape((16, 2 * slots), jnp.int32),
            resident_shape((8, 4 * slots), jnp.int32),
            resident_shape(response.shape),
            resident_shape(base_coeff.shape),
        ]
        + [resident_shape((2, width, unknowns, elements)) for width in WIDTHS[1:]],
        scratch_shapes=[pltpu.VMEM((2 * harm_count * unknowns, 4 * slots), BF16)] * 2
        + [pltpu.SMEM(round_masks.shape, jnp.int32), pltpu.VMEM(trace_mats.shape, F32)]
        + [pltpu.VMEM(send_elem.shape, jnp.int32)] * 3
        + [pltpu.SemaphoreType.DMA((7 + later,))],
    )(*stay(round_masks, response, base_coeff, trace_mats, send_elem, send_face, recv_elem))
    for value in [piece, *pieces]:
        near.append(from_partner(value, "harm", 1))
    for k in range(len(WIDTHS)):
        far.append(lax.ppermute(near[k], "harm", skip))

    small = from_partner(first, "dom", 1)

    def choice(kernel, rows, *values):
        shapes = [resident_shape((n * harm_count, face_vars, 2 * slots)) for n in rows]
        return pl.pallas_call(
            kernel,
            name="choice",
            compiler_params=KERNEL_MEMORY,
            in_specs=[VMEM] * (1 + len(values)),
            out_specs=[VMEM] * len(rows),
            out_shape=shapes,
        )(*resident(lane_bits, *values))

    def stage(value, mask):
        return from_partner(value, "dom", mask)

    part = functools.partial
    kept_x, kept_y = choice(split_kernel, (2, 1), small, first)
    moved_x = stage(kept_x, 2)
    moved_y = stage(kept_y, 12)
    kept_x, rider = choice(part(first_x_kernel, 1), (1, 1), moved_x, kept_x)
    moved_x = stage(kept_x, 4)
    (kept_y,) = choice(part(y_kernel, 3), (1,), moved_y, kept_y)
    moved_y = stage(kept_y, 2)
    (kept_x,) = choice(part(second_x_kernel, 2), (2,), moved_x, kept_x, rider)
    moved_x = stage(kept_x, 12)
    (kept_y,) = choice(part(y_kernel, 1), (1,), moved_y, kept_y)
    moved_y = stage(kept_y, 4)
    (kept,) = choice(part(join_kernel, (3, 2)), (3,), moved_x, kept_x, moved_y, kept_y)
    swapped = stage(kept, 16)

    acc = pl.pallas_call(
        own_kernel,
        name="own",
        compiler_params=KERNEL_MEMORY,
        in_specs=[VMEM] * 2,
        out_specs=VMEM,
        out_shape=resident_shape(response.shape),
    )(*resident(response, base_coeff))

    def near_call(acc, first, chunks):
        return pl.pallas_call(
            lambda *refs: near_kernel(first, *refs),
            name="near",
            compiler_params=KERNEL_MEMORY,
            in_specs=[VMEM] * (2 + len(chunks)),
            out_specs=VMEM,
            out_shape=resident_shape(response.shape),
        )(*resident(base_coeff, acc, *chunks))

    acc = near_call(acc, 0, near[:EARLY])
    acc = near_call(acc, EARLY, near[EARLY:])
    image = pl.pallas_call(
        main_kernel,
        name="main",
        compiler_params=KERNEL_MEMORY,
        in_specs=[VMEM] * (3 + len(WIDTHS)),
        out_specs=VMEM,
        out_shape=resident_shape(response.shape),
        scratch_shapes=[pltpu.VMEM(response.shape, F32)],
    )(*resident(base_coeff, response, acc), volume_mat, *resident(*far[:-1]))
    edge_shape = (2, WIDTHS[-1], unknowns, elements)
    image = pl.pallas_call(
        edge_kernel,
        name="edge",
        compiler_params=KERNEL_MEMORY,
        in_specs=[VMEM] * 4,
        out_specs=VMEM,
        out_shape=resident_shape(response.shape),
        input_output_aliases={3: 0},
        scratch_shapes=[pltpu.VMEM(edge_shape, F32)],
    )(*resident(base_coeff), volume_mat, *resident(far[-1], image))
    return pl.pallas_call(
        lift_kernel,
        name="lift",
        compiler_params=KERNEL_MEMORY,
        in_specs=[VMEM] * 7,
        out_specs=HBM,
        out_shape=shape_like(whole),
        scratch_shapes=[
            pltpu.VMEM((2 * harm_count * face_vars, elements), F32),
            pltpu.VMEM(response.shape, F32),
            pltpu.SemaphoreType.DMA((harm_count,)),
        ],
    )(
        *resident(image), lift_mat.T, *resident(places, lane_bits, small, swapped, kept),
    )


def solution(mesh):
    in_specs = (
        P(None, "harm", None, "dom"),
        P(None, None, None, "dom"),
        P(),
        P(),
        P(),
        P(),
        P(None, "dom"),
        P(None, "dom"),
        P(None, "dom"),
    )
    out_specs = P(None, "harm", None, "dom")

    return jax.shard_map(local, mesh=mesh, in_specs=in_specs, out_specs=out_specs, check_vma=False)
```

profile of v0, /device:TPU:32, one launch (start us, length us, event | category | flops | bytes accessed | tf_op | source)
XLA Modules:
  0.0 54.9 jit_solution(10488043230175534643)
XLA Ops:
  0.0 2.3 %traces.1 = (f32[32,16,128]{2,1,0:T(8,128)S(1)}, s32[16,128]{1,0:T(8,128)S(1)}, s32[8,256]{1,0:T(8,128)S(1)}, f32[2,8,64,256]{3,2,1,0:T(8,128)S(1)}, f32[2,17,64...) custom-call(s32[4]{0:T(128)} %masks_hbm.1, ...), custom_call_target="tpu_custom_call" | custom-call | tf_op jit(solution)/shard_map/traces/pallas_call | solution.py:436
  2.5 1.5 %collective-permute-done.8.swapped.small = f32[32,16,128]{2,1,0:T(8,128)S(1)} collective-permute-done((f32[32,16,128]{2,1,0:T(8,128)S(1)}, f32[32,16,128]{2,1,0:T(8,128)S(1)}, u32[]{:S(2)}, u32[]{:S(2)}) %collective-permute-start.8) | collective-permute-done | bytes 262176 | tf_op jit(solution)/shard_map/ppermute | solution.py:401
  4.0 1.9 %collective-permute-start.9 = (f32[16,16,128]{2,1,0:T(8,128)S(1)}, f32[16,16,128]{2,1,0:T(8,128)S(1)}, u32[]{:S(2)}, u32[]{:S(2)}) collective-permute-start(f32[16,16,128]{2,1,0:T(8,128)S(1)} %get-tuple-element.25.kept), channel_id=1, source_target_pairs={{0,2},{1,3},{2,0},{3,1},{4,6},{5,7},{6,4},{7,5},{8,10},{9,11},{10,... | collective-permute-start | bytes 393224 | tf_op jit(solution)/shard_map/ppermute | solution.py:401
  5.9 4.6 %collective-permute-start.12 = (f32[8,16,128]{2,1,0:T(8,128)S(1)}, f32[8,16,128]{2,1,0:T(8,128)S(1)}, u32[]{:S(2)}, u32[]{:S(2)}) collective-permute-start(f32[8,16,128]{2,1,0:T(8,128)S(1)} %get-tuple-element.28.kept), channel_id=1, source_target_pairs={{0,12},{1,13},{2,14},{3,15},{4,8},{5,9},{6,10},{7,11},{8,4},{9,5},... | collective-permute-start | bytes 196616 | tf_op jit(solution)/shard_map/ppermute | solution.py:401
  10.5 1.6 %collective-permute-start = (f32[2,2,64,256]{3,2,1,0:T(8,128)S(1)}, f32[2,2,64,256]{3,2,1,0:T(8,128)S(1)}, u32[]{:S(2)}, u32[]{:S(2)}) collective-permute-start(f32[2,2,64,256]{3,2,1,0:T(8,128)S(1)} %get-tuple-element.18), channel_id=1, source_target_pairs={{0,32},{32,0},{64,96},{96,64},{128,160},{160,128},{192,224},{224,1... | collective-permute-start | bytes 786440 | tf_op jit(solution)/shard_map/ppermute | solution.py:401
  13.6 1.6 %collective-permute-start.3 = (f32[2,2,64,256]{3,2,1,0:T(8,128)S(1)}, f32[2,2,64,256]{3,2,1,0:T(8,128)S(1)}, u32[]{:S(2)}, u32[]{:S(2)}) collective-permute-start(f32[2,2,64,256]{3,2,1,0:T(8,128)S(1)} %get-tuple-element.20), channel_id=1, source_target_pairs={{0,32},{32,0},{64,96},{96,64},{128,160},{160,128},{192,224},{224,1... | collective-permute-start | bytes 786440 | tf_op jit(solution)/shard_map/ppermute | solution.py:401
  15.6 2.5 %collective-permute-start.13 = (f32[8,16,128]{2,1,0:T(8,128)S(1)}, f32[8,16,128]{2,1,0:T(8,128)S(1)}, u32[]{:S(2)}, u32[]{:S(2)}) collective-permute-start(f32[8,16,128]{2,1,0:T(8,128)S(1)} %choice.9.kept), channel_id=1, source_target_pairs={{0,2},{1,3},{2,0},{3,1},{4,6},{5,7},{6,4},{7,5},{8,10},{9,11},{10,... | collective-permute-start | bytes 196616 | tf_op jit(solution)/shard_map/ppermute | solution.py:401
  18.1 2.2 %collective-permute-done.13.swapped = f32[8,16,128]{2,1,0:T(8,128)S(1)} collective-permute-done((f32[8,16,128]{2,1,0:T(8,128)S(1)}, f32[8,16,128]{2,1,0:T(8,128)S(1)}, u32[]{:S(2)}, u32[]{:S(2)}) %collective-permute-start.13) | collective-permute-done | bytes 65568 | tf_op jit(solution)/shard_map/ppermute | solution.py:401
  20.4 2.5 %collective-permute-start.10 = (f32[8,16,128]{2,1,0:T(8,128)S(1)}, f32[8,16,128]{2,1,0:T(8,128)S(1)}, u32[]{:S(2)}, u32[]{:S(2)}) collective-permute-start(f32[8,16,128]{2,1,0:T(8,128)S(1)} %get-tuple-element.26.kept), channel_id=1, source_target_pairs={{0,4},{1,5},{2,6},{3,7},{4,0},{5,1},{6,2},{7,3},{8,12},{9,13},{10,... | collective-permute-start | bytes 196616 | tf_op jit(solution)/shard_map/ppermute | solution.py:401
  22.8 2.7 %collective-permute-done.10.swapped = f32[8,16,128]{2,1,0:T(8,128)S(1)} collective-permute-done((f32[8,16,128]{2,1,0:T(8,128)S(1)}, f32[8,16,128]{2,1,0:T(8,128)S(1)}, u32[]{:S(2)}, u32[]{:S(2)}) %collective-permute-start.10) | collective-permute-done | bytes 65568 | tf_op jit(solution)/shard_map/ppermute | solution.py:401
  25.5 3.4 %collective-permute-start.14 = (f32[8,16,128]{2,1,0:T(8,128)S(1)}, f32[8,16,128]{2,1,0:T(8,128)S(1)}, u32[]{:S(2)}, u32[]{:S(2)}) collective-permute-start(f32[8,16,128]{2,1,0:T(8,128)S(1)} %choice.10.kept_y), channel_id=1, source_target_pairs={{0,4},{1,5},{2,6},{3,7},{4,0},{5,1},{6,2},{7,3},{8,12},{9,13},{10,... | collective-permute-start | bytes 196616 | tf_op jit(solution)/shard_map/ppermute | solution.py:401
  28.9 1.7 %collective-permute-start.11 = (f32[16,16,128]{2,1,0:T(8,128)S(1)}, f32[16,16,128]{2,1,0:T(8,128)S(1)}, u32[]{:S(2)}, u32[]{:S(2)}) collective-permute-start(f32[16,16,128]{2,1,0:T(8,128)S(1)} %choice.8.kept_x), channel_id=1, source_target_pairs={{0,12},{1,13},{2,14},{3,15},{4,8},{5,9},{6,10},{7,11},{8,4},{9,5},... | collective-permute-start | bytes 393224 | tf_op jit(solution)/shard_map/ppermute | solution.py:401
  30.7 1.5 %collective-permute-start.5 = (f32[2,2,64,256]{3,2,1,0:T(8,128)S(1)}, f32[2,2,64,256]{3,2,1,0:T(8,128)S(1)}, u32[]{:S(2)}, u32[]{:S(2)}) collective-permute-start(f32[2,2,64,256]{3,2,1,0:T(8,128)S(1)} %collective-permute-done.2.refs_2_), channel_id=1, source_target_pairs={{0,64},{32,224},{64,128},{96,32},{128,192},{160,96},{192,0},{224,1... | collective-permute-start | bytes 786440 | tf_op jit(solution)/shard_map/ppermute | solution.py:458
  32.2 1.5 %collective-permute-start.6 = (f32[2,2,64,256]{3,2,1,0:T(8,128)S(1)}, f32[2,2,64,256]{3,2,1,0:T(8,128)S(1)}, u32[]{:S(2)}, u32[]{:S(2)}) collective-permute-start(f32[2,2,64,256]{3,2,1,0:T(8,128)S(1)} %collective-permute-done.3.refs_3_), channel_id=1, source_target_pairs={{0,64},{32,224},{64,128},{96,32},{128,192},{160,96},{192,0},{224,1... | collective-permute-start | bytes 786440 | tf_op jit(solution)/shard_map/ppermute | solution.py:458
  33.6 1.5 %collective-permute-done.4.refs_2_ = f32[2,2,64,256]{3,2,1,0:T(8,128)S(1)} collective-permute-done((f32[2,2,64,256]{3,2,1,0:T(8,128)S(1)}, f32[2,2,64,256]{3,2,1,0:T(8,128)S(1)}, u32[]{:S(2)}, u32[]{:S(2)}) %collective-permute-start.4) | collective-permute-done | bytes 262176 | tf_op jit(solution)/shard_map/ppermute | solution.py:401
  35.1 1.5 %collective-permute-start.7 = (f32[2,2,64,256]{3,2,1,0:T(8,128)S(1)}, f32[2,2,64,256]{3,2,1,0:T(8,128)S(1)}, u32[]{:S(2)}, u32[]{:S(2)}) collective-permute-start(f32[2,2,64,256]{3,2,1,0:T(8,128)S(1)} %collective-permute-done.4.refs_2_), channel_id=1, source_target_pairs={{0,64},{32,224},{64,128},{96,32},{128,192},{160,96},{192,0},{224,1... | collective-permute-start | bytes 786440 | tf_op jit(solution)/shard_map/ppermute | solution.py:458
  36.6 1.5 %collective-permute-start.1 = (f32[2,2,64,256]{3,2,1,0:T(8,128)S(1)}, f32[2,2,64,256]{3,2,1,0:T(8,128)S(1)}, u32[]{:S(2)}, u32[]{:S(2)}) collective-permute-start(f32[2,2,64,256]{3,2,1,0:T(8,128)S(1)} %collective-permute-done.refs_3_), channel_id=1, source_target_pairs={{0,64},{32,224},{64,128},{96,32},{128,192},{160,96},{192,0},{224,1... | collective-permute-start | bytes 786440 | tf_op jit(solution)/shard_map/ppermute | solution.py:458
  38.2 3.3 %collective-permute-start.15 = (f32[24,16,128]{2,1,0:T(8,128)S(1)}, f32[24,16,128]{2,1,0:T(8,128)S(1)}, u32[]{:S(2)}, u32[]{:S(2)}) collective-permute-start(f32[24,16,128]{2,1,0:T(8,128)S(1)} %choice.11.kept), channel_id=1, source_target_pairs={{0,16},{1,17},{2,18},{3,19},{4,20},{5,21},{6,22},{7,23},{8,24},{9,... | collective-permute-start | bytes 589832 | tf_op jit(solution)/shard_map/ppermute | solution.py:401
  41.4 1.4 %own.1.refs_1_ = f32[2,8,64,256]{3,2,1,0:T(8,128)S(1)} custom-call(f32[2,8,64,256]{3,2,1,0:T(8,128)S(1)} %get-tuple-element.19.response, f32[2,17,64,256]{3,2,1,0:T(8,128)S(1)} %get-tuple-element.17.coeff.refs_0_), custom_call_target="tpu_custom_call" | custom-call | tf_op jit(solution)/shard_map/own/pallas_call | solution.py:491
  44.1 1.4 %collective-permute-done.6.refs_1_ = f32[2,2,64,256]{3,2,1,0:T(8,128)S(1)} collective-permute-done((f32[2,2,64,256]{3,2,1,0:T(8,128)S(1)}, f32[2,2,64,256]{3,2,1,0:T(8,128)S(1)}, u32[]{:S(2)}, u32[]{:S(2)}) %collective-permute-start.6) | collective-permute-done | bytes 262176 | tf_op jit(solution)/shard_map/ppermute | solution.py:458
  45.6 4.5 %collective-permute-done.7.refs_2_ = f32[2,2,64,256]{3,2,1,0:T(8,128)S(1)} collective-permute-done((f32[2,2,64,256]{3,2,1,0:T(8,128)S(1)}, f32[2,2,64,256]{3,2,1,0:T(8,128)S(1)}, u32[]{:S(2)}, u32[]{:S(2)}) %collective-permute-start.7) | collective-permute-done | bytes 262176 | tf_op jit(solution)/shard_map/ppermute | solution.py:458
  50.0 1.3 %main.1.image = f32[2,8,64,256]{3,2,1,0:T(8,128)S(1)} custom-call(f32[2,17,64,256]{3,2,1,0:T(8,128)S(1)} %get-tuple-element.17.coeff.refs_0_, f32[2,8,64,256]{3,2,1,0:T(8,128)S(1)} %get-tuple-element.19.response, f32[2,8,64,256]{3,2,1,0:T(8,128)S(1)} %near.3.acc, f32[64,64]{1,0:T(8,128)S(1)} %copy-done, ...), custom_call_target="tpu_custom_call" | custom-call | tf_op jit(solution)/shard_map/main/pallas_call | solution.py:512
  51.4 1.5 %collective-permute-done.1.chunk = f32[2,2,64,256]{3,2,1,0:T(8,128)S(1)} collective-permute-done((f32[2,2,64,256]{3,2,1,0:T(8,128)S(1)}, f32[2,2,64,256]{3,2,1,0:T(8,128)S(1)}, u32[]{:S(2)}, u32[]{:S(2)}) %collective-permute-start.1) | collective-permute-done | bytes 262176 | tf_op jit(solution)/shard_map/ppermute | solution.py:458
  53.4 1.5 %lift.1 = f32[2,8,64,256]{3,2,1,0:T(8,128)} custom-call(f32[2,8,64,256]{3,2,1,0:T(8,128)S(1)} %edge.1.image, f32[16,64]{1,0:T(8,128)S(1)} %bitcast.1, s32[8,256]{1,0:T(8,128)S(1)} %get-tuple-element.22.places, s32[16,128]{1,0:T(8,128)S(1)} %get-tuple-element.23.lane_bits, f32[32,16,128]{2,1,0:T(8,128)S(1)} %collective-permute-done.8.swapped.small, ...), custom_call_target="tpu_custom_call" | custom-call | tf_op jit(solution)/shard_map/lift/pallas_call | solution.py:532
  (26 shorter events, 4.0 us)
Async XLA Ops:
  2.4 1.6 %collective-permute-start.8 = (f32[32,16,128]{2,1,0:T(8,128)S(1)}, f32[32,16,128]{2,1,0:T(8,128)S(1)}, u32[]{:S(2)}, u32[]{:S(2)}) collective-permute-start(f32[32,16,128]{2,1,0:T(8,128)S(1)} %get-tuple-element.24.kept), channel_id=1, source_target_pairs={{0,1},{1,0},{2,3},{3,2},{4,5},{5,4},{6,7},{7,6},{8,9},{9,8},{10,11... | collective-permute-start | bytes 786440 | tf_op jit(solution)/shard_map/ppermute | solution.py:401
  4.0 11.6 %collective-permute-start.9 = (f32[16,16,128]{2,1,0:T(8,128)S(1)}, f32[16,16,128]{2,1,0:T(8,128)S(1)}, u32[]{:S(2)}, u32[]{:S(2)}) collective-permute-start(f32[16,16,128]{2,1,0:T(8,128)S(1)} %get-tuple-element.25.kept), channel_id=1, source_target_pairs={{0,2},{1,3},{2,0},{3,1},{4,6},{5,7},{6,4},{7,5},{8,10},{9,11},{10,... | collective-permute-start | bytes 393224 | tf_op jit(solution)/shard_map/ppermute | solution.py:401
  5.9 9.3 %collective-permute-start.12 = (f32[8,16,128]{2,1,0:T(8,128)S(1)}, f32[8,16,128]{2,1,0:T(8,128)S(1)}, u32[]{:S(2)}, u32[]{:S(2)}) collective-permute-start(f32[8,16,128]{2,1,0:T(8,128)S(1)} %get-tuple-element.28.kept), channel_id=1, source_target_pairs={{0,12},{1,13},{2,14},{3,15},{4,8},{5,9},{6,10},{7,11},{8,4},{9,5},... | collective-permute-start | bytes 196616 | tf_op jit(solution)/shard_map/ppermute | solution.py:401
  10.5 18.4 %collective-permute-start = (f32[2,2,64,256]{3,2,1,0:T(8,128)S(1)}, f32[2,2,64,256]{3,2,1,0:T(8,128)S(1)}, u32[]{:S(2)}, u32[]{:S(2)}) collective-permute-start(f32[2,2,64,256]{3,2,1,0:T(8,128)S(1)} %get-tuple-element.18), channel_id=1, source_target_pairs={{0,32},{32,0},{64,96},{96,64},{128,160},{160,128},{192,224},{224,1... | collective-permute-start | bytes 786440 | tf_op jit(solution)/shard_map/ppermute | solution.py:401
  13.0 17.6 %collective-permute-start.2 = (f32[2,2,64,256]{3,2,1,0:T(8,128)S(1)}, f32[2,2,64,256]{3,2,1,0:T(8,128)S(1)}, u32[]{:S(2)}, u32[]{:S(2)}) collective-permute-start(f32[2,2,64,256]{3,2,1,0:T(8,128)S(1)} %cut.1), channel_id=1, source_target_pairs={{0,32},{32,0},{64,96},{96,64},{128,160},{160,128},{192,224},{224,1... | collective-permute-start | bytes 786440 | tf_op jit(solution)/shard_map/ppermute | solution.py:401
  13.6 18.6 %collective-permute-start.3 = (f32[2,2,64,256]{3,2,1,0:T(8,128)S(1)}, f32[2,2,64,256]{3,2,1,0:T(8,128)S(1)}, u32[]{:S(2)}, u32[]{:S(2)}) collective-permute-start(f32[2,2,64,256]{3,2,1,0:T(8,128)S(1)} %get-tuple-element.20), channel_id=1, source_target_pairs={{0,32},{32,0},{64,96},{96,64},{128,160},{160,128},{192,224},{224,1... | collective-permute-start | bytes 786440 | tf_op jit(solution)/shard_map/ppermute | solution.py:401
  15.2 20.0 %collective-permute-start.4 = (f32[2,2,64,256]{3,2,1,0:T(8,128)S(1)}, f32[2,2,64,256]{3,2,1,0:T(8,128)S(1)}, u32[]{:S(2)}, u32[]{:S(2)}) collective-permute-start(f32[2,2,64,256]{3,2,1,0:T(8,128)S(1)} %get-tuple-element.21), channel_id=1, source_target_pairs={{0,32},{32,0},{64,96},{96,64},{128,160},{160,128},{192,224},{224,1... | collective-permute-start | bytes 786440 | tf_op jit(solution)/shard_map/ppermute | solution.py:401
  15.6 4.7 %collective-permute-start.13 = (f32[8,16,128]{2,1,0:T(8,128)S(1)}, f32[8,16,128]{2,1,0:T(8,128)S(1)}, u32[]{:S(2)}, u32[]{:S(2)}) collective-permute-start(f32[8,16,128]{2,1,0:T(8,128)S(1)} %choice.9.kept), channel_id=1, source_target_pairs={{0,2},{1,3},{2,0},{3,1},{4,6},{5,7},{6,4},{7,5},{8,10},{9,11},{10,... | collective-permute-start | bytes 196616 | tf_op jit(solution)/shard_map/ppermute | solution.py:401
  20.4 5.2 %collective-permute-start.10 = (f32[8,16,128]{2,1,0:T(8,128)S(1)}, f32[8,16,128]{2,1,0:T(8,128)S(1)}, u32[]{:S(2)}, u32[]{:S(2)}) collective-permute-start(f32[8,16,128]{2,1,0:T(8,128)S(1)} %get-tuple-element.26.kept), channel_id=1, source_target_pairs={{0,4},{1,5},{2,6},{3,7},{4,0},{5,1},{6,2},{7,3},{8,12},{9,13},{10,... | collective-permute-start | bytes 196616 | tf_op jit(solution)/shard_map/ppermute | solution.py:401
  25.5 11.1 %collective-permute-start.14 = (f32[8,16,128]{2,1,0:T(8,128)S(1)}, f32[8,16,128]{2,1,0:T(8,128)S(1)}, u32[]{:S(2)}, u32[]{:S(2)}) collective-permute-start(f32[8,16,128]{2,1,0:T(8,128)S(1)} %choice.10.kept_y), channel_id=1, source_target_pairs={{0,4},{1,5},{2,6},{3,7},{4,0},{5,1},{6,2},{7,3},{8,12},{9,13},{10,... | collective-permute-start | bytes 196616 | tf_op jit(solution)/shard_map/ppermute | solution.py:401
  28.9 9.2 %collective-permute-start.11 = (f32[16,16,128]{2,1,0:T(8,128)S(1)}, f32[16,16,128]{2,1,0:T(8,128)S(1)}, u32[]{:S(2)}, u32[]{:S(2)}) collective-permute-start(f32[16,16,128]{2,1,0:T(8,128)S(1)} %choice.8.kept_x), channel_id=1, source_target_pairs={{0,12},{1,13},{2,14},{3,15},{4,8},{5,9},{6,10},{7,11},{8,4},{9,5},... | collective-permute-start | bytes 393224 | tf_op jit(solution)/shard_map/ppermute | solution.py:401
  30.7 13.5 %collective-permute-start.5 = (f32[2,2,64,256]{3,2,1,0:T(8,128)S(1)}, f32[2,2,64,256]{3,2,1,0:T(8,128)S(1)}, u32[]{:S(2)}, u32[]{:S(2)}) collective-permute-start(f32[2,2,64,256]{3,2,1,0:T(8,128)S(1)} %collective-permute-done.2.refs_2_), channel_id=1, source_target_pairs={{0,64},{32,224},{64,128},{96,32},{128,192},{160,96},{192,0},{224,1... | collective-permute-start | bytes 786440 | tf_op jit(solution)/shard_map/ppermute | solution.py:458
  32.2 13.4 %collective-permute-start.6 = (f32[2,2,64,256]{3,2,1,0:T(8,128)S(1)}, f32[2,2,64,256]{3,2,1,0:T(8,128)S(1)}, u32[]{:S(2)}, u32[]{:S(2)}) collective-permute-start(f32[2,2,64,256]{3,2,1,0:T(8,128)S(1)} %collective-permute-done.3.refs_3_), channel_id=1, source_target_pairs={{0,64},{32,224},{64,128},{96,32},{128,192},{160,96},{192,0},{224,1... | collective-permute-start | bytes 786440 | tf_op jit(solution)/shard_map/ppermute | solution.py:458
  35.1 14.9 %collective-permute-start.7 = (f32[2,2,64,256]{3,2,1,0:T(8,128)S(1)}, f32[2,2,64,256]{3,2,1,0:T(8,128)S(1)}, u32[]{:S(2)}, u32[]{:S(2)}) collective-permute-start(f32[2,2,64,256]{3,2,1,0:T(8,128)S(1)} %collective-permute-done.4.refs_2_), channel_id=1, source_target_pairs={{0,64},{32,224},{64,128},{96,32},{128,192},{160,96},{192,0},{224,1... | collective-permute-start | bytes 786440 | tf_op jit(solution)/shard_map/ppermute | solution.py:458
  36.6 16.2 %collective-permute-start.1 = (f32[2,2,64,256]{3,2,1,0:T(8,128)S(1)}, f32[2,2,64,256]{3,2,1,0:T(8,128)S(1)}, u32[]{:S(2)}, u32[]{:S(2)}) collective-permute-start(f32[2,2,64,256]{3,2,1,0:T(8,128)S(1)} %collective-permute-done.refs_3_), channel_id=1, source_target_pairs={{0,64},{32,224},{64,128},{96,32},{128,192},{160,96},{192,0},{224,1... | collective-permute-start | bytes 786440 | tf_op jit(solution)/shard_map/ppermute | solution.py:458
  38.2 15.2 %collective-permute-start.15 = (f32[24,16,128]{2,1,0:T(8,128)S(1)}, f32[24,16,128]{2,1,0:T(8,128)S(1)}, u32[]{:S(2)}, u32[]{:S(2)}) collective-permute-start(f32[24,16,128]{2,1,0:T(8,128)S(1)} %choice.11.kept), channel_id=1, source_target_pairs={{0,16},{1,17},{2,18},{3,19},{4,20},{5,21},{6,22},{7,23},{8,24},{9,... | collective-permute-start | bytes 589832 | tf_op jit(solution)/shard_map/ppermute | solution.py:401
  43.4 6.7 %copy-start = (f32[64,64]{1,0:T(8,128)S(1)}, f32[64,64]{1,0:T(8,128)}, u32[]{:S(2)}) copy-start(f32[64,64]{1,0:T(8,128)} %volume_mat.3) | copy-start | bytes 49156
  51.4 2.1 %copy-start.1 = (f32[64,16]{0,1:T(8,128)S(1)}, f32[64,16]{0,1:T(8,128)}, u32[]{:S(2)}) copy-start(f32[64,16]{0,1:T(8,128)} %param.13) | copy-start | bytes 12292
where the time goes:
time: 55 us; the launch traced here: 54.9 us
  starting transfers between devices  30 us (55%)
  waiting for transfers between devices  15.4 us (28%)
  Pallas kernels  9.39 us (17%)
    ppermute x12, starting transfers between devices, from_partner(): lax.ppermute(value, axis, [(i, i ^ mask) for i in range(lax.axis_size(axi...  24 us
    ppermute x12, waiting for transfers between devices, from_partner(): lax.ppermute(value, axis, [(i, i ^ mask) for i in range(lax.axis_size(axi...  7.97 us
    ppermute x4, waiting for transfers between devices, local(): far.append(lax.ppermute(near[k], 'harm', skip))  7.39 us
    ppermute x4, starting transfers between devices, local(): far.append(lax.ppermute(near[k], 'harm', skip))  5.97 us
    pallas_call x1, Pallas kernels, local(): pl.pallas_call(trace_kernel, name='traces', compiler_params=KERNEL_MEMORY...  2.34 us
    pallas_call x1, Pallas kernels, local(): pl.pallas_call(lift_kernel, name='lift', compiler_params=KERNEL_MEMORY, i...  1.49 us
    pallas_call x1, Pallas kernels, local(): pl.pallas_call(own_kernel, name='own', compiler_params=KERNEL_MEMORY, in_...  1.39 us
    pallas_call x1, Pallas kernels, local(): pl.pallas_call(main_kernel, name='main', compiler_params=KERNEL_MEMORY, i...  1.31 us
  transfers between devices with their start and end apart: 16, of which 7 were waited for; matrix products, arithmetic and copies ran while one was open for 0% of the time, Pallas kernels for 10%

commit v1 on v0

--- a/solution.py
+++ b/solution.py
@@ -11,6 +11,8 @@
 REACH = 8
 ROUNDS = 4
 WIDTHS = (2, 2, 2, 2)
+FAR_WIDTHS = (2, 2, 2, 1, 1)
+FAR_EARLY = 3
 EARLY = 2
 base_omega = 0.2
 
@@ -59,12 +61,12 @@
     return jnp.concatenate([ref[pl.ds(r, 1), :] for r in rows], axis=1)
 
 
-def piece_copy(response, k, piece, sem):
+def piece_copy(response, k, piece, sem, widths=WIDTHS):
     count = response.shape[1]
     odd = lax.axis_index("harm") % 2
-    upward, downward = (chunk_harmonics(k, count, way)[0] for way in (True, False))
+    upward, downward = (chunk_harmonics(k, count, way, widths)[0] for way in (True, False))
     first = jnp.where(odd == 1, downward, upward)
-    return pltpu.make_async_copy(response.at[:, pl.ds(first, WIDTHS[k])], piece, sem)
+    return pltpu.make_async_copy(response.at[:, pl.ds(first, widths[k])], piece, sem)
 
 
 def cut_kernel(response, piece, sem):
@@ -73,11 +75,16 @@
     copy.wait()
 
 
+def relay_kernel(chunk, out):
+    odd = lax.axis_index("harm") % 2
+    out[...] = chunk[:, pl.ds(1 - odd, 1)]
+
+
 def trace_kernel(masks_hbm, response_hbm, coeff_hbm, mats_hbm, elem_hbm, face_hbm, recv_hbm, *refs):
     count = len(WIDTHS) - 1
-    first, lane_bits, places, response, coeff = refs[:5]
-    pieces = refs[5:5 + count]
-    p_high, p_low, masks, trace_mats, send_elem, send_face, recv_elem, sems = refs[5 + count:]
+    first, lane_bits, places, response, coeff, direct = refs[:6]
+    pieces = refs[6:6 + count]
+    p_high, p_low, masks, trace_mats, send_elem, send_face, recv_elem, sems = refs[6 + count:]
     fetched = (
         (response_hbm, response), (masks_hbm, masks), (elem_hbm, send_elem), (face_hbm, send_face),
         (mats_hbm, trace_mats), (recv_hbm, recv_elem),
@@ -90,6 +97,11 @@
         for k, piece in enumerate(pieces, 1)
     ]
     copies.append(pltpu.make_async_copy(coeff_hbm, coeff, sems.at[len(fetched)]))
+    copies.append(
+        piece_copy(
+            response_hbm, len(FAR_WIDTHS) - 1, direct, sems.at[len(fetched) + count + 1], FAR_WIDTHS
+        )
+    )
     for copy in fetches + copies:
         copy.start()
     for copy in fetches[1:]:
@@ -216,17 +228,17 @@
     return REACH + j - i
 
 
-def chunk_harmonics(k, count, ascending):
-    done = sum(WIDTHS[:k])
-    first = done if ascending else count - done - WIDTHS[k]
-    return [first + q for q in range(WIDTHS[k])]
-
-
-def gather_sources(chunks, first, count, ascending, index):
+def chunk_harmonics(k, count, ascending, widths=WIDTHS):
+    done = sum(widths[:k])
+    first = done if ascending else count - done - widths[k]
+    return [first + q for q in range(widths[k])]
+
+
+def gather_sources(chunks, first, count, ascending, index, widths):
     return [
         (chunk, q, i, index)
         for k, chunk in enumerate(chunks)
-        for q, i in enumerate(chunk_harmonics(first + k, count, ascending))
+        for q, i in enumerate(chunk_harmonics(first + k, count, ascending, widths))
     ]
 
 
@@ -272,7 +284,7 @@
     harm_count, unknowns, elements = acc.shape[1:]
 
     def run(ascending, near_index, far_index):
-        sources = gather_sources(chunks, first, harm_count, ascending, near_index)
+        sources = gather_sources(chunks, first, harm_count, ascending, near_index, WIDTHS)
 
         def body(r, e):
             start = lambda j: (acc[0, j, r, e], acc[1, j, r, e])
@@ -299,7 +311,7 @@
     harm_count, unknowns, elements = acc.shape[1:]
 
     def run(ascending, near_index, far_index):
-        sources = gather_sources(chunks, 0, harm_count, ascending, far_index)
+        sources = gather_sources(chunks, 0, harm_count, ascending, far_index, FAR_WIDTHS)
 
         def body(r, e):
             start = lambda j: (acc[0, j, r, e], acc[1, j, r, e])
@@ -362,14 +374,15 @@
         copy.wait()
 
 
-def edge_kernel(coeff, volume_mat, chunk, image, out, conv):
-    width, unknowns, elements = chunk.shape[1:]
+def edge_kernel(coeff, volume_mat, relayed, direct, image, out, conv):
+    width, unknowns, elements = conv.shape[1:]
     harm_count = out.shape[1]
-    last = len(WIDTHS) - 1
     stack = stacked(volume_mat[...])
 
     def run(ascending, near_index, far_index):
-        sources = gather_sources([chunk], last, harm_count, ascending, far_index)
+        sources = gather_sources(
+            [relayed, direct], FAR_EARLY, harm_count, ascending, far_index, FAR_WIDTHS
+        )
         first = harm_count - width if ascending else 0
         outputs = range(first, first + width)
 
@@ -433,29 +446,40 @@
         scratch_shapes=[pltpu.SemaphoreType.DMA],
     )(*stay(response))
     later = len(WIDTHS) - 1
-    first, lane_bits, places, response, base_coeff, *pieces = pl.pallas_call(
+    first, lane_bits, places, response, base_coeff, direct, *pieces = pl.pallas_call(
         trace_kernel,
         name="traces",
         compiler_params=KERNEL_MEMORY,
         in_specs=[HBM] * 7,
-        out_specs=[VMEM] * (5 + later),
+        out_specs=[VMEM] * (6 + later),
         out_shape=[
             resident_shape((4 * harm_count, face_vars, 2 * slots)),
             resident_shape((16, 2 * slots), jnp.int32),
             resident_shape((8, 4 * slots), jnp.int32),
             resident_shape(response.shape),
             resident_shape(base_coeff.shape),
+            resident_shape((2, 1, unknowns, elements)),
         ]
         + [resident_shape((2, width, unknowns, elements)) for width in WIDTHS[1:]],
         scratch_shapes=[pltpu.VMEM((2 * harm_count * unknowns, 4 * slots), BF16)] * 2
         + [pltpu.SMEM(round_masks.shape, jnp.int32), pltpu.VMEM(trace_mats.shape, F32)]
         + [pltpu.VMEM(send_elem.shape, jnp.int32)] * 3
-        + [pltpu.SemaphoreType.DMA((7 + later,))],
+        + [pltpu.SemaphoreType.DMA((8 + later,))],
     )(*stay(round_masks, response, base_coeff, trace_mats, send_elem, send_face, recv_elem))
     for value in [piece, *pieces]:
         near.append(from_partner(value, "harm", 1))
-    for k in range(len(WIDTHS)):
-        far.append(lax.ppermute(near[k], "harm", skip))
+    relayed = pl.pallas_call(
+        relay_kernel,
+        name="relay",
+        compiler_params=KERNEL_MEMORY,
+        in_specs=[VMEM],
+        out_specs=VMEM,
+        out_shape=resident_shape((2, 1, unknowns, elements)),
+    )(*resident(near[-1]))
+    for value in [*near[:-1], relayed]:
+        far.append(lax.ppermute(value, "harm", skip))
+    across = [(i, (i + 1) % groups if i % 2 == 1 else (i - 1) % groups) for i in range(groups)]
+    far.append(lax.ppermute(direct, "harm", across))
 
     small = from_partner(first, "dom", 1)
 
@@ -513,22 +537,22 @@
         main_kernel,
         name="main",
         compiler_params=KERNEL_MEMORY,
-        in_specs=[VMEM] * (3 + len(WIDTHS)),
+        in_specs=[VMEM] * (4 + FAR_EARLY),
         out_specs=VMEM,
         out_shape=resident_shape(response.shape),
         scratch_shapes=[pltpu.VMEM(response.shape, F32)],
-    )(*resident(base_coeff, response, acc), volume_mat, *resident(*far[:-1]))
-    edge_shape = (2, WIDTHS[-1], unknowns, elements)
+    )(*resident(base_coeff, response, acc), volume_mat, *resident(*far[:FAR_EARLY]))
+    edge_shape = (2, sum(FAR_WIDTHS[FAR_EARLY:]), unknowns, elements)
     image = pl.pallas_call(
         edge_kernel,
         name="edge",
         compiler_params=KERNEL_MEMORY,
-        in_specs=[VMEM] * 4,
+        in_specs=[VMEM] * 5,
         out_specs=VMEM,
         out_shape=resident_shape(response.shape),
-        input_output_aliases={3: 0},
+        input_output_aliases={4: 0},
         scratch_shapes=[pltpu.VMEM(edge_shape, F32)],
-    )(*resident(base_coeff), volume_mat, *resident(far[-1], image))
+    )(*resident(base_coeff), volume_mat, *resident(*far[FAR_EARLY:], image))
     return pl.pallas_call(
         lift_kernel,
         name="lift",

time: 55 us -> 47 us (0.85)
  the two profiles are of different devices: /device:TPU:32 before, /device:TPU:6 now
where the time goes in v1:
time: 47 us; the launch traced here: 46.8 us
  starting transfers between devices  29.9 us (64%)
  Pallas kernels  9.45 us (20%)
  waiting for transfers between devices  7.18 us (15%)
    ppermute x12, starting transfers between devices, from_partner(): lax.ppermute(value, axis, [(i, i ^ mask) for i in range(lax.axis_size(axi...  25.6 us
    ppermute x12, waiting for transfers between devices, from_partner(): lax.ppermute(value, axis, [(i, i ^ mask) for i in range(lax.axis_size(axi...  7.17 us
    ppermute x4, starting transfers between devices, local(): far.append(lax.ppermute(value, 'harm', skip))  3.92 us
    pallas_call x1, Pallas kernels, local(): pl.pallas_call(trace_kernel, name='traces', compiler_params=KERNEL_MEMORY...  2.35 us
    pallas_call x1, Pallas kernels, local(): pl.pallas_call(lift_kernel, name='lift', compiler_params=KERNEL_MEMORY, i...  1.48 us
    pallas_call x1, Pallas kernels, local(): pl.pallas_call(own_kernel, name='own', compiler_params=KERNEL_MEMORY, in_...  1.39 us
    pallas_call x1, Pallas kernels, local(): pl.pallas_call(main_kernel, name='main', compiler_params=KERNEL_MEMORY, i...  1.34 us
    pallas_call x2, Pallas kernels, near_call(): pl.pallas_call(lambda *refs: near_kernel(first, *refs), name='near', comp...  1.25 us
  transfers between devices with their start and end apart: 17, of which 4 were waited for; matrix products, arithmetic and copies ran while one was open for 0% of the time, Pallas kernels for 12%

profile of v1, /device:TPU:6, one launch (start us, length us, event | category | flops | bytes accessed | tf_op | source)
XLA Modules:
  0.0 46.8 jit_solution(9083120633776330376)
XLA Ops:
  0.0 2.4 %traces.1 = (f32[32,16,128]{2,1,0:T(8,128)S(1)}, s32[16,128]{1,0:T(8,128)S(1)}, s32[8,256]{1,0:T(8,128)S(1)}, f32[2,8,64,256]{3,2,1,0:T(8,128)S(1)}, f32[2,17,64...) custom-call(s32[4]{0:T(128)} %masks_hbm.1, ...), custom_call_target="tpu_custom_call" | custom-call | tf_op jit(solution)/shard_map/traces/pallas_call | solution.py:449
  2.5 1.0 %cut.1 = f32[2,2,64,256]{3,2,1,0:T(8,128)S(1)} custom-call(f32[2,8,64,256]{3,2,1,0:T(8,128)} %response.1), custom_call_target="tpu_custom_call" | custom-call | tf_op jit(solution)/shard_map/cut/pallas_call | solution.py:439
  3.4 1.7 %collective-permute-start.3 = (f32[2,2,64,256]{3,2,1,0:T(8,128)S(1)}, f32[2,2,64,256]{3,2,1,0:T(8,128)S(1)}, u32[]{:S(2)}, u32[]{:S(2)}) collective-permute-start(f32[2,2,64,256]{3,2,1,0:T(8,128)S(1)} %cut.1), channel_id=1, source_target_pairs={{0,32},{32,0},{64,96},{96,64},{128,160},{160,128},{192,224},{224,1... | collective-permute-start | bytes 786440 | tf_op jit(solution)/shard_map/ppermute | solution.py:414
  5.6 2.0 %collective-permute-start.10 = (f32[16,16,128]{2,1,0:T(8,128)S(1)}, f32[16,16,128]{2,1,0:T(8,128)S(1)}, u32[]{:S(2)}, u32[]{:S(2)}) collective-permute-start(f32[16,16,128]{2,1,0:T(8,128)S(1)} %get-tuple-element.27.kept), channel_id=1, source_target_pairs={{0,2},{1,3},{2,0},{3,1},{4,6},{5,7},{6,4},{7,5},{8,10},{9,11},{10,... | collective-permute-start | bytes 393224 | tf_op jit(solution)/shard_map/ppermute | solution.py:414
  7.6 1.6 %collective-permute-start.5 = (f32[2,2,64,256]{3,2,1,0:T(8,128)S(1)}, f32[2,2,64,256]{3,2,1,0:T(8,128)S(1)}, u32[]{:S(2)}, u32[]{:S(2)}) collective-permute-start(f32[2,2,64,256]{3,2,1,0:T(8,128)S(1)} %get-tuple-element.23), channel_id=1, source_target_pairs={{0,32},{32,0},{64,96},{96,64},{128,160},{160,128},{192,224},{224,1... | collective-permute-start | bytes 786440 | tf_op jit(solution)/shard_map/ppermute | solution.py:414
  9.2 5.4 %collective-permute-start.13 = (f32[8,16,128]{2,1,0:T(8,128)S(1)}, f32[8,16,128]{2,1,0:T(8,128)S(1)}, u32[]{:S(2)}, u32[]{:S(2)}) collective-permute-start(f32[8,16,128]{2,1,0:T(8,128)S(1)} %get-tuple-element.30.kept), channel_id=1, source_target_pairs={{0,12},{1,13},{2,14},{3,15},{4,8},{5,9},{6,10},{7,11},{8,4},{9,5},... | collective-permute-start | bytes 196616 | tf_op jit(solution)/shard_map/ppermute | solution.py:414
  14.6 3.1 %collective-permute-done.13.swapped = f32[8,16,128]{2,1,0:T(8,128)S(1)} collective-permute-done((f32[8,16,128]{2,1,0:T(8,128)S(1)}, f32[8,16,128]{2,1,0:T(8,128)S(1)}, u32[]{:S(2)}, u32[]{:S(2)}) %collective-permute-start.13) | collective-permute-done | bytes 65568 | tf_op jit(solution)/shard_map/ppermute | solution.py:414
  17.7 0.7 %collective-permute-start.14 = (f32[8,16,128]{2,1,0:T(8,128)S(1)}, f32[8,16,128]{2,1,0:T(8,128)S(1)}, u32[]{:S(2)}, u32[]{:S(2)}) collective-permute-start(f32[8,16,128]{2,1,0:T(8,128)S(1)} %choice.9.kept), channel_id=1, source_target_pairs={{0,2},{1,3},{2,0},{3,1},{4,6},{5,7},{6,4},{7,5},{8,10},{9,11},{10,... | collective-permute-start | bytes 196616 | tf_op jit(solution)/shard_map/ppermute | solution.py:414
  18.4 2.0 %collective-permute-start.11 = (f32[8,16,128]{2,1,0:T(8,128)S(1)}, f32[8,16,128]{2,1,0:T(8,128)S(1)}, u32[]{:S(2)}, u32[]{:S(2)}) collective-permute-start(f32[8,16,128]{2,1,0:T(8,128)S(1)} %get-tuple-element.28.kept), channel_id=1, source_target_pairs={{0,4},{1,5},{2,6},{3,7},{4,0},{5,1},{6,2},{7,3},{8,12},{9,13},{10,... | collective-permute-start | bytes 196616 | tf_op jit(solution)/shard_map/ppermute | solution.py:414
  20.5 1.5 %collective-permute-start = (f32[2,2,64,256]{3,2,1,0:T(8,128)S(1)}, f32[2,2,64,256]{3,2,1,0:T(8,128)S(1)}, u32[]{:S(2)}, u32[]{:S(2)}) collective-permute-start(f32[2,2,64,256]{3,2,1,0:T(8,128)S(1)} %get-tuple-element.19), channel_id=1, source_target_pairs={{0,32},{32,0},{64,96},{96,64},{128,160},{160,128},{192,224},{224,1... | collective-permute-start | bytes 786440 | tf_op jit(solution)/shard_map/ppermute | solution.py:414
  22.1 0.5 %collective-permute-start.6 = (f32[2,2,64,256]{3,2,1,0:T(8,128)S(1)}, f32[2,2,64,256]{3,2,1,0:T(8,128)S(1)}, u32[]{:S(2)}, u32[]{:S(2)}) collective-permute-start(f32[2,2,64,256]{3,2,1,0:T(8,128)S(1)} %collective-permute-done.3.refs_2_), channel_id=1, source_target_pairs={{0,64},{32,224},{64,128},{96,32},{128,192},{160,96},{192,0},{224,1... | collective-permute-start | bytes 786440 | tf_op jit(solution)/shard_map/ppermute | solution.py:480
  22.5 1.1 %collective-permute-done.11.swapped = f32[8,16,128]{2,1,0:T(8,128)S(1)} collective-permute-done((f32[8,16,128]{2,1,0:T(8,128)S(1)}, f32[8,16,128]{2,1,0:T(8,128)S(1)}, u32[]{:S(2)}, u32[]{:S(2)}) %collective-permute-start.11) | collective-permute-done | bytes 65568 | tf_op jit(solution)/shard_map/ppermute | solution.py:414
  23.7 2.0 %collective-permute-start.15 = (f32[8,16,128]{2,1,0:T(8,128)S(1)}, f32[8,16,128]{2,1,0:T(8,128)S(1)}, u32[]{:S(2)}, u32[]{:S(2)}) collective-permute-start(f32[8,16,128]{2,1,0:T(8,128)S(1)} %choice.10.kept_y), channel_id=1, source_target_pairs={{0,4},{1,5},{2,6},{3,7},{4,0},{5,1},{6,2},{7,3},{8,12},{9,13},{10,... | collective-permute-start | bytes 196616 | tf_op jit(solution)/shard_map/ppermute | solution.py:414
  25.7 5.3 %collective-permute-start.12 = (f32[16,16,128]{2,1,0:T(8,128)S(1)}, f32[16,16,128]{2,1,0:T(8,128)S(1)}, u32[]{:S(2)}, u32[]{:S(2)}) collective-permute-start(f32[16,16,128]{2,1,0:T(8,128)S(1)} %choice.8.kept_x), channel_id=1, source_target_pairs={{0,12},{1,13},{2,14},{3,15},{4,8},{5,9},{6,10},{7,11},{8,4},{9,5},... | collective-permute-start | bytes 393224 | tf_op jit(solution)/shard_map/ppermute | solution.py:414
  31.1 1.0 %collective-permute-start.8 = (f32[2,2,64,256]{3,2,1,0:T(8,128)S(1)}, f32[2,2,64,256]{3,2,1,0:T(8,128)S(1)}, u32[]{:S(2)}, u32[]{:S(2)}) collective-permute-start(f32[2,2,64,256]{3,2,1,0:T(8,128)S(1)} %collective-permute-done.5.refs_2_), channel_id=1, source_target_pairs={{0,64},{32,224},{64,128},{96,32},{128,192},{160,96},{192,0},{224,1... | collective-permute-start | bytes 786440 | tf_op jit(solution)/shard_map/ppermute | solution.py:480
  32.0 2.8 %collective-permute-done.12.swapped_x = f32[16,16,128]{2,1,0:T(8,128)S(1)} collective-permute-done((f32[16,16,128]{2,1,0:T(8,128)S(1)}, f32[16,16,128]{2,1,0:T(8,128)S(1)}, u32[]{:S(2)}, u32[]{:S(2)}) %collective-permute-start.12) | collective-permute-done | bytes 131104 | tf_op jit(solution)/shard_map/ppermute | solution.py:414
  34.8 2.9 %collective-permute-start.16 = (f32[24,16,128]{2,1,0:T(8,128)S(1)}, f32[24,16,128]{2,1,0:T(8,128)S(1)}, u32[]{:S(2)}, u32[]{:S(2)}) collective-permute-start(f32[24,16,128]{2,1,0:T(8,128)S(1)} %choice.11.kept), channel_id=1, source_target_pairs={{0,16},{1,17},{2,18},{3,19},{4,20},{5,21},{6,22},{7,23},{8,24},{9,... | collective-permute-start | bytes 589832 | tf_op jit(solution)/shard_map/ppermute | solution.py:414
  38.1 2.5 %collective-permute-start.1 = (f32[2,1,64,256]{3,2,1,0:T(8,128)S(1)}, f32[2,1,64,256]{3,2,1,0:T(8,128)S(1)}, u32[]{:S(2)}, u32[]{:S(2)}) collective-permute-start(f32[2,1,64,256]{3,2,1,0:T(8,128)S(1)} %relay.1), channel_id=1, source_target_pairs={{0,64},{32,224},{64,128},{96,32},{128,192},{160,96},{192,0},{224,1... | collective-permute-start | bytes 393224 | tf_op jit(solution)/shard_map/ppermute | solution.py:480
  40.5 1.4 %own.1.refs_1_ = f32[2,8,64,256]{3,2,1,0:T(8,128)S(1)} custom-call(f32[2,8,64,256]{3,2,1,0:T(8,128)S(1)} %get-tuple-element.21.response, f32[2,17,64,256]{3,2,1,0:T(8,128)S(1)} %get-tuple-element.18.coeff.refs_0_), custom_call_target="tpu_custom_call" | custom-call | tf_op jit(solution)/shard_map/own/pallas_call | solution.py:515
  41.9 0.5 %near.2.refs_1_ = f32[2,8,64,256]{3,2,1,0:T(8,128)S(1)} custom-call(f32[2,17,64,256]{3,2,1,0:T(8,128)S(1)} %get-tuple-element.18.coeff.refs_0_, f32[2,8,64,256]{3,2,1,0:T(8,128)S(1)} %own.1.refs_1_, f32[2,2,64,256]{3,2,1,0:T(8,128)S(1)} %collective-permute-done.3.refs_2_, f32[2,2,64,256]{3,2,1,0:T(8,128)S(1)} %collective-permute-done.4.refs_3_), custom_call_target="tpu_custom_call" | custom-call | tf_op jit(solution)/shard_map/near/pallas_call | solution.py:525
  42.5 0.7 %near.3.acc = f32[2,8,64,256]{3,2,1,0:T(8,128)S(1)} custom-call(f32[2,17,64,256]{3,2,1,0:T(8,128)S(1)} %get-tuple-element.18.coeff.refs_0_, f32[2,8,64,256]{3,2,1,0:T(8,128)S(1)} %near.2.refs_1_, f32[2,2,64,256]{3,2,1,0:T(8,128)S(1)} %collective-permute-done.5.refs_2_, f32[2,2,64,256]{3,2,1,0:T(8,128)S(1)} %collective-permute-done.chunk.refs_3_), custom_call_target="tpu_custom_call" | custom-call | tf_op jit(solution)/shard_map/near/pallas_call | solution.py:525
  43.3 1.3 %main.1.image = f32[2,8,64,256]{3,2,1,0:T(8,128)S(1)} custom-call(f32[2,17,64,256]{3,2,1,0:T(8,128)S(1)} %get-tuple-element.18.coeff.refs_0_, f32[2,8,64,256]{3,2,1,0:T(8,128)S(1)} %get-tuple-element.21.response, f32[2,8,64,256]{3,2,1,0:T(8,128)S(1)} %near.3.acc, f32[64,64]{1,0:T(8,128)S(1)} %copy-done, ...), custom_call_target="tpu_custom_call" | custom-call | tf_op jit(solution)/shard_map/main/pallas_call | solution.py:536
  44.6 0.5 %edge.1.image = f32[2,8,64,256]{3,2,1,0:T(8,128)S(1)} custom-call(f32[2,17,64,256]{3,2,1,0:T(8,128)S(1)} %get-tuple-element.18.coeff.refs_0_, f32[64,64]{1,0:T(8,128)S(1)} %copy-done, f32[2,1,64,256]{3,2,1,0:T(8,128)S(1)} %collective-permute-done.1.relayed, f32[2,1,64,256]{3,2,1,0:T(8,128)S(1)} %collective-permute-done.2.direct, ...), custom_call_target="tpu_custom_call", output_to_operand_aliasing={{}: (4, {})} | custom-call | tf_op jit(solution)/shard_map/edge/pallas_call | solution.py:546
  45.3 1.5 %lift.1 = f32[2,8,64,256]{3,2,1,0:T(8,128)} custom-call(f32[2,8,64,256]{3,2,1,0:T(8,128)S(1)} %edge.1.image, f32[16,64]{1,0:T(8,128)S(1)} %bitcast.1, s32[8,256]{1,0:T(8,128)S(1)} %get-tuple-element.24.places, s32[16,128]{1,0:T(8,128)S(1)} %get-tuple-element.25.lane_bits, f32[32,16,128]{2,1,0:T(8,128)S(1)} %collective-permute-done.9.swapped.small, ...), custom_call_target="tpu_custom_call" | custom-call | tf_op jit(solution)/shard_map/lift/pallas_call | solution.py:556
  (29 shorter events, 1.2 us)
Async XLA Ops:
  2.4 3.2 %collective-permute-start.9 = (f32[32,16,128]{2,1,0:T(8,128)S(1)}, f32[32,16,128]{2,1,0:T(8,128)S(1)}, u32[]{:S(2)}, u32[]{:S(2)}) collective-permute-start(f32[32,16,128]{2,1,0:T(8,128)S(1)} %get-tuple-element.26.kept), channel_id=1, source_target_pairs={{0,1},{1,0},{2,3},{3,2},{4,5},{5,4},{6,7},{7,6},{8,9},{9,8},{10,11... | collective-permute-start | bytes 786440 | tf_op jit(solution)/shard_map/ppermute | solution.py:414
  3.4 17.0 %collective-permute-start.3 = (f32[2,2,64,256]{3,2,1,0:T(8,128)S(1)}, f32[2,2,64,256]{3,2,1,0:T(8,128)S(1)}, u32[]{:S(2)}, u32[]{:S(2)}) collective-permute-start(f32[2,2,64,256]{3,2,1,0:T(8,128)S(1)} %cut.1), channel_id=1, source_target_pairs={{0,32},{32,0},{64,96},{96,64},{128,160},{160,128},{192,224},{224,1... | collective-permute-start | bytes 786440 | tf_op jit(solution)/shard_map/ppermute | solution.py:414
  5.1 20.6 %collective-permute-start.4 = (f32[2,2,64,256]{3,2,1,0:T(8,128)S(1)}, f32[2,2,64,256]{3,2,1,0:T(8,128)S(1)}, u32[]{:S(2)}, u32[]{:S(2)}) collective-permute-start(f32[2,2,64,256]{3,2,1,0:T(8,128)S(1)} %get-tuple-element.22), channel_id=1, source_target_pairs={{0,32},{32,0},{64,96},{96,64},{128,160},{160,128},{192,224},{224,1... | collective-permute-start | bytes 786440 | tf_op jit(solution)/shard_map/ppermute | solution.py:414
  5.6 12.8 %collective-permute-start.10 = (f32[16,16,128]{2,1,0:T(8,128)S(1)}, f32[16,16,128]{2,1,0:T(8,128)S(1)}, u32[]{:S(2)}, u32[]{:S(2)}) collective-permute-start(f32[16,16,128]{2,1,0:T(8,128)S(1)} %get-tuple-element.27.kept), channel_id=1, source_target_pairs={{0,2},{1,3},{2,0},{3,1},{4,6},{5,7},{6,4},{7,5},{8,10},{9,11},{10,... | collective-permute-start | bytes 393224 | tf_op jit(solution)/shard_map/ppermute | solution.py:414
  7.6 23.5 %collective-permute-start.5 = (f32[2,2,64,256]{3,2,1,0:T(8,128)S(1)}, f32[2,2,64,256]{3,2,1,0:T(8,128)S(1)}, u32[]{:S(2)}, u32[]{:S(2)}) collective-permute-start(f32[2,2,64,256]{3,2,1,0:T(8,128)S(1)} %get-tuple-element.23), channel_id=1, source_target_pairs={{0,32},{32,0},{64,96},{96,64},{128,160},{160,128},{192,224},{224,1... | collective-permute-start | bytes 786440 | tf_op jit(solution)/shard_map/ppermute | solution.py:414
  9.2 8.5 %collective-permute-start.13 = (f32[8,16,128]{2,1,0:T(8,128)S(1)}, f32[8,16,128]{2,1,0:T(8,128)S(1)}, u32[]{:S(2)}, u32[]{:S(2)}) collective-permute-start(f32[8,16,128]{2,1,0:T(8,128)S(1)} %get-tuple-element.30.kept), channel_id=1, source_target_pairs={{0,12},{1,13},{2,14},{3,15},{4,8},{5,9},{6,10},{7,11},{8,4},{9,5},... | collective-permute-start | bytes 196616 | tf_op jit(solution)/shard_map/ppermute | solution.py:414
  17.7 4.4 %collective-permute-start.14 = (f32[8,16,128]{2,1,0:T(8,128)S(1)}, f32[8,16,128]{2,1,0:T(8,128)S(1)}, u32[]{:S(2)}, u32[]{:S(2)}) collective-permute-start(f32[8,16,128]{2,1,0:T(8,128)S(1)} %choice.9.kept), channel_id=1, source_target_pairs={{0,2},{1,3},{2,0},{3,1},{4,6},{5,7},{6,4},{7,5},{8,10},{9,11},{10,... | collective-permute-start | bytes 196616 | tf_op jit(solution)/shard_map/ppermute | solution.py:414
  18.4 5.3 %collective-permute-start.11 = (f32[8,16,128]{2,1,0:T(8,128)S(1)}, f32[8,16,128]{2,1,0:T(8,128)S(1)}, u32[]{:S(2)}, u32[]{:S(2)}) collective-permute-start(f32[8,16,128]{2,1,0:T(8,128)S(1)} %get-tuple-element.28.kept), channel_id=1, source_target_pairs={{0,4},{1,5},{2,6},{3,7},{4,0},{5,1},{6,2},{7,3},{8,12},{9,13},{10,... | collective-permute-start | bytes 196616 | tf_op jit(solution)/shard_map/ppermute | solution.py:414
  20.5 17.3 %collective-permute-start = (f32[2,2,64,256]{3,2,1,0:T(8,128)S(1)}, f32[2,2,64,256]{3,2,1,0:T(8,128)S(1)}, u32[]{:S(2)}, u32[]{:S(2)}) collective-permute-start(f32[2,2,64,256]{3,2,1,0:T(8,128)S(1)} %get-tuple-element.19), channel_id=1, source_target_pairs={{0,32},{32,0},{64,96},{96,64},{128,160},{160,128},{192,224},{224,1... | collective-permute-start | bytes 786440 | tf_op jit(solution)/shard_map/ppermute | solution.py:414
  22.1 16.0 %collective-permute-start.6 = (f32[2,2,64,256]{3,2,1,0:T(8,128)S(1)}, f32[2,2,64,256]{3,2,1,0:T(8,128)S(1)}, u32[]{:S(2)}, u32[]{:S(2)}) collective-permute-start(f32[2,2,64,256]{3,2,1,0:T(8,128)S(1)} %collective-permute-done.3.refs_2_), channel_id=1, source_target_pairs={{0,64},{32,224},{64,128},{96,32},{128,192},{160,96},{192,0},{224,1... | collective-permute-start | bytes 786440 | tf_op jit(solution)/shard_map/ppermute | solution.py:480
  23.7 7.4 %collective-permute-start.15 = (f32[8,16,128]{2,1,0:T(8,128)S(1)}, f32[8,16,128]{2,1,0:T(8,128)S(1)}, u32[]{:S(2)}, u32[]{:S(2)}) collective-permute-start(f32[8,16,128]{2,1,0:T(8,128)S(1)} %choice.10.kept_y), channel_id=1, source_target_pairs={{0,4},{1,5},{2,6},{3,7},{4,0},{5,1},{6,2},{7,3},{8,12},{9,13},{10,... | collective-permute-start | bytes 196616 | tf_op jit(solution)/shard_map/ppermute | solution.py:414
  25.7 9.1 %collective-permute-start.12 = (f32[16,16,128]{2,1,0:T(8,128)S(1)}, f32[16,16,128]{2,1,0:T(8,128)S(1)}, u32[]{:S(2)}, u32[]{:S(2)}) collective-permute-start(f32[16,16,128]{2,1,0:T(8,128)S(1)} %choice.8.kept_x), channel_id=1, source_target_pairs={{0,12},{1,13},{2,14},{3,15},{4,8},{5,9},{6,10},{7,11},{8,4},{9,5},... | collective-permute-start | bytes 393224 | tf_op jit(solution)/shard_map/ppermute | solution.py:414
  31.1 12.2 %collective-permute-start.7 = (f32[2,2,64,256]{3,2,1,0:T(8,128)S(1)}, f32[2,2,64,256]{3,2,1,0:T(8,128)S(1)}, u32[]{:S(2)}, u32[]{:S(2)}) collective-permute-start(f32[2,2,64,256]{3,2,1,0:T(8,128)S(1)} %collective-permute-done.4.refs_3_), channel_id=1, source_target_pairs={{0,64},{32,224},{64,128},{96,32},{128,192},{160,96},{192,0},{224,1... | collective-permute-start | bytes 786440 | tf_op jit(solution)/shard_map/ppermute | solution.py:480
  31.1 12.2 %collective-permute-start.8 = (f32[2,2,64,256]{3,2,1,0:T(8,128)S(1)}, f32[2,2,64,256]{3,2,1,0:T(8,128)S(1)}, u32[]{:S(2)}, u32[]{:S(2)}) collective-permute-start(f32[2,2,64,256]{3,2,1,0:T(8,128)S(1)} %collective-permute-done.5.refs_2_), channel_id=1, source_target_pairs={{0,64},{32,224},{64,128},{96,32},{128,192},{160,96},{192,0},{224,1... | collective-permute-start | bytes 786440 | tf_op jit(solution)/shard_map/ppermute | solution.py:480
  34.8 10.4 %collective-permute-start.16 = (f32[24,16,128]{2,1,0:T(8,128)S(1)}, f32[24,16,128]{2,1,0:T(8,128)S(1)}, u32[]{:S(2)}, u32[]{:S(2)}) collective-permute-start(f32[24,16,128]{2,1,0:T(8,128)S(1)} %choice.11.kept), channel_id=1, source_target_pairs={{0,16},{1,17},{2,18},{3,19},{4,20},{5,21},{6,22},{7,23},{8,24},{9,... | collective-permute-start | bytes 589832 | tf_op jit(solution)/shard_map/ppermute | solution.py:414
  37.7 6.9 %collective-permute-start.2 = (f32[2,1,64,256]{3,2,1,0:T(8,128)S(1)}, f32[2,1,64,256]{3,2,1,0:T(8,128)S(1)}, u32[]{:S(2)}, u32[]{:S(2)}) collective-permute-start(f32[2,1,64,256]{3,2,1,0:T(8,128)S(1)} %get-tuple-element.20), channel_id=1, source_target_pairs={{0,224},{32,64},{64,32},{96,128},{128,96},{160,192},{192,160},{224... | collective-permute-start | bytes 393224 | tf_op jit(solution)/shard_map/ppermute | solution.py:482
  38.1 6.6 %collective-permute-start.1 = (f32[2,1,64,256]{3,2,1,0:T(8,128)S(1)}, f32[2,1,64,256]{3,2,1,0:T(8,128)S(1)}, u32[]{:S(2)}, u32[]{:S(2)}) collective-permute-start(f32[2,1,64,256]{3,2,1,0:T(8,128)S(1)} %relay.1), channel_id=1, source_target_pairs={{0,64},{32,224},{64,128},{96,32},{128,192},{160,96},{192,0},{224,1... | collective-permute-start | bytes 393224 | tf_op jit(solution)/shard_map/ppermute | solution.py:480
  42.5 0.8 %copy-start = (f32[64,64]{1,0:T(8,128)S(1)}, f32[64,64]{1,0:T(8,128)}, u32[]{:S(2)}) copy-start(f32[64,64]{1,0:T(8,128)} %volume_mat.3) | copy-start | bytes 49156
  44.6 0.7 %copy-start.1 = (f32[64,16]{0,1:T(8,128)S(1)}, f32[64,16]{0,1:T(8,128)}, u32[]{:S(2)}) copy-start(f32[64,16]{0,1:T(8,128)} %param.13) | copy-start | bytes 12292
